TPU v7x, 32 devices: a whole 2x2x4 slice. The times are simulated.
32 devices in a mesh: parts: 2 (over y), mp: 4 (over z), shot: 4 (over x, core).
Axes of the slice: x: 2, y: 2, z: 4, core: 2. Of those that a mesh axis runs over, the one named last changes fastest.
Arguments:
- courant: float32 [192, 256, 128], P(('parts', 'mp')), parts along dimension 0, may hold values from 0.04 to 0.2
- forward_old: float32 [8, 96, 256, 128], P(('parts', 'shot'), 'mp'), parts along dimension 0, may hold values from -5 to 5
- forward_now: float32 [8, 96, 256, 128], P(('parts', 'shot'), 'mp'), parts along dimension 0, may hold values from -5 to 5
- adjoint_late: float32 [8, 96, 256, 128], P(('parts', 'shot'), 'mp'), parts along dimension 0, may hold values from -5 to 5
- adjoint_now: float32 [8, 96, 256, 128], P(('parts', 'shot'), 'mp'), parts along dimension 0, may hold values from -5 to 5
- src_cell: int32 [8, 64], P(('parts', 'shot')), parts along dimension 0, may hold values from 0 to 3145727
- src_sign: int32 [8, 64], P(('parts', 'shot')), parts along dimension 0, may hold values from 0 to 1
- wavelet: float32 [8, 2, 64], P(('parts', 'shot')), parts along dimension 0, may hold values from -16 to 16
- rec_cell: int32 [4096], P('parts'), parts along dimension 0, may hold values from 0 to 3145727
- rec_data: float32 [8, 2, 2048], P(('parts', 'shot')), parts along dimension 0, may hold values from -16 to 16
Outputs:
- raw_gradient: float32 [192, 256, 128], P(('parts', 'mp'), 'shot'), parts along dimension 0
- smooth_gradient: float32 [192, 256, 128], P(('parts', 'shot'), None, 'mp'), parts along dimension 0
There are 2 independent parts, one for each index of `parts`. A program takes and returns all parts, laid end to end along the dimension named above; each array names one. Nothing has to cross between parts.
All inputs are finite; a program needn't handle non-finite values.
Results may differ from a plain program's by a relative error of at most 0.00025.
Values sent between devices are 32-bit elements; how exact they have to be, the bound alone decides.
A program may use at most 128 MiB of HBM per device.

v0:
```python
import functools
import math

import jax
import jax.numpy as jnp
import numpy as np
from jax import lax
from jax.experimental import pallas as pl
from jax.experimental.pallas import tpu as pltpu
from jax.sharding import PartitionSpec as P

SMOOTH_X = 32
SMOOTH_YZ = 4
COEFS = (8.0 / 5.0, -1.0 / 5.0, 8.0 / 315.0, -1.0 / 560.0)
CENTER = -205.0 / 72.0
REACH = 4
HIGHEST = lax.Precision.HIGHEST

VMEM_GRANT = 60 * 2**20


def smoothing_table(length, strength):
    counter = np.arange(1, length + 1, dtype=np.float64)
    sines = np.sin(np.pi * np.outer(counter, counter) / (length + 1))
    half_sine = np.sin(np.pi * counter / (2 * (length + 1)))
    resp = 1.0 / (1.0 + strength * 4.0 * half_sine**2)
    table = 2.0 / (length + 1) * (sines * resp[None, :]) @ sines
    return table, 1.0 / math.sqrt(np.mean(resp * resp))


def stencil_table(length, center):
    table = np.eye(length) * center
    for offset, weight in enumerate(COEFS):
        reach = offset + 1
        if reach < length:
            table += weight * (np.eye(length, k=reach) + np.eye(length, k=-reach))
    return table


def split_table(table):
    high = jnp.asarray(table, jnp.float32).astype(jnp.bfloat16)
    rest = table - np.asarray(high.astype(jnp.float32), np.float64)
    return np.asarray(high), np.asarray(jnp.asarray(rest, jnp.float32).astype(jnp.bfloat16))


def stencil_tables(width_y, width_z):
    with jax.ensure_compile_time_eval():
        y_high, y_low = split_table(stencil_table(width_y, 3.0 * CENTER))
        z_high, z_low = split_table(np.kron(np.eye(2), stencil_table(width_z, 0.0)))
    table_y = np.concatenate([y_high, y_high, y_low], axis=1)
    table_z = np.concatenate([z_high, z_high, z_low], axis=0)
    return table_y, table_z


def scatter_kernel(
    rec_cell, rec_first, rec_second, src_cell, src_first, src_second, base, *outs
):
    *outs, rec_list, src_list = outs
    source_0, source_1, data_0, data_1 = outs
    rows, width = source_0.shape
    zero = jnp.zeros(source_0.shape, jnp.float32)
    for out in outs:
        out[...] = zero
    lanes = lax.broadcasted_iota(jnp.int32, (1, width), 1)
    first_cell = base[0]

    def add_all(cells, first, second, found, out_first, out_second):
        count = cells.shape[0]
        unroll = math.gcd(count, 16)

        def keep(step, kept):
            for extra in range(unroll):
                item = step * unroll + extra
                local = cells[item] - first_cell
                found[kept] = item
                kept += jnp.where((local >= 0) & (local < rows * width), 1, 0)
            return kept

        kept = lax.fori_loop(0, count // unroll, keep, 0)

        def add_one(step, carry):
            item = found[step]
            local = cells[item] - first_cell
            row = local // width
            hit = lanes == local - row * width
            out_first[pl.ds(row, 1), :] += jnp.where(hit, first[item], 0.0)
            out_second[pl.ds(row, 1), :] += jnp.where(hit, second[item], 0.0)
            return carry

        lax.fori_loop(0, kept, add_one, 0)

    add_all(rec_cell, rec_first, rec_second, rec_list, data_0, data_1)
    add_all(src_cell, src_first, src_second, src_list, source_0, source_1)


def injections(src, rec, first_cell, shape):
    flat = jax.ShapeDtypeStruct((shape[0] * shape[1], shape[2]), jnp.float32)
    outs = pl.pallas_call(
        scatter_kernel,
        out_shape=(flat,) * 4,
        in_specs=[pl.BlockSpec(memory_space=pltpu.SMEM)] * 7,
        out_specs=(pl.BlockSpec(memory_space=pltpu.VMEM),) * 4,
        scratch_shapes=[
            pltpu.SMEM((rec[0].shape[0] + 16,), jnp.int32),
            pltpu.SMEM((src[0].shape[0] + 16,), jnp.int32),
        ],
        compiler_params=pltpu.CompilerParams(vmem_limit_bytes=VMEM_GRANT),
        cost_estimate=pl.CostEstimate(flops=0, bytes_accessed=40 * 2**20, transcendentals=0),
        name="inject",
    )(*rec, *src, first_cell)
    return [out.reshape(shape) for out in outs]


def slab_laplace(place, fields, table_y, table_z):
    count = fields[0].shape[0]
    both = jnp.concatenate([field[place] for field in fields], axis=1)
    high = both.astype(jnp.bfloat16)
    low = (both - high.astype(jnp.float32)).astype(jnp.bfloat16)
    total = jnp.dot(
        table_y[...],
        jnp.concatenate([high, low, high], axis=0),
        preferred_element_type=jnp.float32,
    ) + jnp.dot(
        jnp.concatenate([high, low, high], axis=1),
        table_z[...],
        preferred_element_type=jnp.float32,
    )
    width = fields[0].shape[2]
    laps = [total[:, side * width : (side + 1) * width] for side in range(2)]
    for offset, weight in enumerate(COEFS):
        for shift in (offset + 1, -(offset + 1)):
            other = place + shift
            inside = (other >= 0) & (other < count)
            factor = jnp.where(inside, weight, 0.0).astype(jnp.float32)
            other = jnp.clip(other, 0, count - 1)
            laps = [lap + factor * field[other] for lap, field in zip(laps, fields)]
    return laps


def first_kernel(
    f_now, a_now, courant, f_old, a_late, source, data, table_y, table_z, accel, f_next, a_mid
):
    for row in range(REACH):
        place = pl.program_id(0) * REACH + row
        lap_f, lap_a = slab_laplace(place, (f_now, a_now), table_y, table_z)
        here = courant[row]
        accel_row = here * lap_f + source[row]
        accel[row] = accel_row
        f_next[row] = (2.0 * f_now[place] - f_old[row]) + accel_row
        a_mid[row] = (2.0 * a_now[place] - a_late[row]) + (here * lap_a + data[row])


def second_kernel(
    f_now, a_now, courant, a_old, accel, source, data, table_y, table_z, term
):
    for row in range(REACH):
        place = pl.program_id(0) * REACH + row
        lap_f, lap_a = slab_laplace(place, (f_now, a_now), table_y, table_z)
        here = courant[row]
        accel_second = here * lap_f + source[row]
        a_row = a_now[place]
        a_first = (2.0 * a_row - a_old[row]) + (here * lap_a + data[row])
        term[row] = a_first * accel[row] + a_row * accel_second


def slab_step(kernel, outs, field_f, field_a, others, tables):
    rows, width_y, width_z = field_f.shape
    blocks = rows // REACH
    block = (REACH, width_y, width_z)
    here = pl.BlockSpec(block, lambda i: (i, 0, 0))
    field = pl.BlockSpec(field_f.shape, lambda i: (0, 0, 0))
    whole = [pl.BlockSpec(table.shape, lambda i: (0, 0)) for table in tables]
    shape = jax.ShapeDtypeStruct(field_f.shape, jnp.float32)
    return pl.pallas_call(
        kernel,
        grid=(blocks,),
        out_shape=(shape,) * outs,
        in_specs=[field] * 2 + [here] * len(others) + whole,
        out_specs=(here,) * outs,
        compiler_params=pltpu.CompilerParams(
            dimension_semantics=("arbitrary",), vmem_limit_bytes=VMEM_GRANT
        ),
        cost_estimate=pl.CostEstimate(
            flops=2**33, bytes_accessed=40 * 2**20, transcendentals=0
        ),
    )(field_f, field_a, *others, *tables)


def halo_terms(side, row, halo, field):
    total = None
    for offset, weight in enumerate(COEFS):
        reach = offset + 1
        plane = row - reach + REACH if side == 0 else row + reach - REACH
        if 0 <= plane < REACH:
            part = weight * halo[field, plane]
            total = part if total is None else total + part
    return total


def first_edge_kernel(
    halo_low, halo_high, courant, accel_in, next_in, mid_in, accel, f_next, a_mid, low, high
):
    for side, halo, edge in ((0, halo_low, low), (1, halo_high, high)):

        @pl.when(pl.program_id(0) == side)
        def _():
            for row in range(REACH):
                here = courant[row]
                add_f = here * halo_terms(side, row, halo, 0)
                add_a = here * halo_terms(side, row, halo, 1)
                accel[row] = accel_in[row] + add_f
                next_row = next_in[row] + add_f
                mid_row = mid_in[row] + add_a
                f_next[row] = next_row
                a_mid[row] = mid_row
                edge[0, row] = next_row
                edge[1, row] = mid_row


def second_edge_kernel(halo_low, halo_high, courant, accel, a_mid, term, edge):
    for side, halo in ((0, halo_low), (1, halo_high)):

        @pl.when(pl.program_id(0) == side)
        def _():
            for row in range(REACH):
                here = courant[row]
                add_f = here * halo_terms(side, row, halo, 0)
                add_a = here * halo_terms(side, row, halo, 1)
                edge[row] = term[row] + (add_a * accel[row] + a_mid[row] * add_f)


def edge_specs(shape):
    last = shape[0] // REACH - 1
    block = (REACH,) + shape[1:]
    both = pl.BlockSpec((2,) + block, lambda i: (0, 0, 0, 0))
    edge = pl.BlockSpec(block, lambda i: (i * last, 0, 0))
    side = pl.BlockSpec(block, lambda i: (i, 0, 0))
    return both, edge, side


EDGE_PARAMS = dict(dimension_semantics=("arbitrary",), vmem_limit_bytes=VMEM_GRANT)


def first_edges(low, high, courant, accel, f_next, a_mid):
    both, edge, _ = edge_specs(courant.shape)
    full = jax.ShapeDtypeStruct(courant.shape, jnp.float32)
    pair = jax.ShapeDtypeStruct(low.shape, jnp.float32)
    return pl.pallas_call(
        first_edge_kernel,
        grid=(2,),
        out_shape=(full, full, full, pair, pair),
        in_specs=[both, both, edge, edge, edge, edge],
        out_specs=(edge, edge, edge, both, both),
        input_output_aliases={3: 0, 4: 1, 5: 2},
        compiler_params=pltpu.CompilerParams(**EDGE_PARAMS),
        name="first_edges",
    )(low, high, courant, accel, f_next, a_mid)


def second_edges(low, high, courant, accel, a_mid, term):
    both, edge, side = edge_specs(courant.shape)
    shape = jax.ShapeDtypeStruct((2 * REACH,) + courant.shape[1:], jnp.float32)
    return pl.pallas_call(
        second_edge_kernel,
        grid=(2,),
        out_shape=shape,
        in_specs=[both, both, edge, edge, edge, edge],
        out_specs=side,
        compiler_params=pltpu.CompilerParams(**EDGE_PARAMS),
        name="second_edges",
    )(low, high, courant, accel, a_mid, term)


def pack_kernel(f_low, f_high, a_low, a_high, low, high):
    low[0], low[1] = f_low[...], a_low[...]
    high[0], high[1] = f_high[...], a_high[...]


def pack_edges(field_f, field_a):
    block = (REACH,) + field_f.shape[1:]
    last = field_f.shape[0] // REACH - 1
    low = pl.BlockSpec(block, lambda i: (0, 0, 0))
    high = pl.BlockSpec(block, lambda i: (last, 0, 0))
    both = pl.BlockSpec((2,) + block, lambda i: (0, 0, 0, 0))
    pair = jax.ShapeDtypeStruct((2,) + block, jnp.float32)
    return pl.pallas_call(
        pack_kernel,
        grid=(1,),
        out_shape=(pair, pair),
        in_specs=[low, high, low, high],
        out_specs=(both, both),
        compiler_params=pltpu.CompilerParams(vmem_limit_bytes=VMEM_GRANT),
        name="pack_edges",
    )(field_f, field_f, field_a, field_a)


def exchange(low_edge, high_edge):
    count = lax.axis_size("mp")
    upward = [(i, i + 1) for i in range(count - 1)]
    downward = [(i + 1, i) for i in range(count - 1)]
    from_low = lax.ppermute(high_edge, "mp", upward)
    from_high = lax.ppermute(low_edge, "mp", downward)
    return from_low, from_high


def sum_groups(term):
    count = lax.axis_size("shot")
    place = lax.axis_index("shot")
    rows, width_y, width_z = term.shape
    part = term.reshape(rows, count, width_y // count, width_z)
    bit = 1
    while bit < count:
        split = part.reshape(rows, part.shape[1] // 2, 2, part.shape[2], width_z)
        own = (place // bit) % 2
        mine = lax.dynamic_index_in_dim(split, own, 2, keepdims=False)
        other = lax.dynamic_index_in_dim(split, 1 - own, 2, keepdims=False)
        sent = lax.ppermute(other, "shot", [(i, i ^ bit) for i in range(count)])
        part = mine + sent
        bit *= 2
    return part[:, 0]


def slab_tables(table, count):
    rows = table.shape[0] // count
    local, sums, gains = [], [], []
    for me in range(count):
        own = slice(me * rows, (me + 1) * rows)
        local.append(table[own, own])
        sums.append(np.stack([table[me * rows, own], table[(me + 1) * rows - 1, own]]))
        gain = []
        for shift in range(1, count):
            source = (me - shift) % count
            seen = (source + 1) * rows - 1 if source < me else source * rows
            gain.append(table[own, seen] / table[seen, seen])
        gains.append(np.stack(gain, axis=1) if gain else np.zeros((rows, 0)))
    mix = np.concatenate([np.stack(local), np.stack(gains)], axis=2)
    return mix.astype(np.float32), np.stack(sums).astype(np.float32)


def mean_kernel(groups, inner, outer, sums, raw, planes):
    rows, edge = raw.shape[0], outer.shape[0] // 2
    total = [None, None]
    for row in range(rows):
        if row < edge:
            plane = outer[row]
        elif row < rows - edge:
            plane = inner[row - edge]
        else:
            plane = outer[row - rows + 2 * edge]
        plane = plane / groups
        raw[row] = plane
        for side in range(2):
            part = sums[side, row] * plane
            total[side] = part if row == 0 else total[side] + part
    planes[0], planes[1] = total


def make_smooth_kernel(count, group, lines):
    def kernel(raw, *refs):
        planes, (mix, table_z) = refs[: count - 1], refs[count - 1 : count + 1]
        pieces, mixed = refs[count + 1 : -1], refs[-1]
        rows = raw.shape[0]
        step = math.gcd(rows, 4)

        def some(index, carry):
            base = index * step
            sums = [None] * step
            for source in range(rows + count - 1):
                plane = raw[source] if source < rows else planes[source - rows][0]
                for extra in range(step):
                    part = mix[base + extra, source] * plane
                    sums[extra] = part if source == 0 else sums[extra] + part
            for extra in range(step):
                mixed[base + extra] = sums[extra]
            return carry

        lax.fori_loop(0, rows // step, some, 0)
        apart = rows // group
        for place in range(apart):
            stacked = jnp.concatenate(
                [mixed[part * apart + place] for part in range(group)], axis=0
            )
            turned = lax.dot_general(
                table_z[...],
                stacked,
                (((1,), (1,)), ((), ())),
                precision=HIGHEST,
                preferred_element_type=jnp.float32,
            )
            for target, piece in enumerate(pieces):
                piece[place] = turned[target * lines : (target + 1) * lines]

    return kernel


def make_last_kernel(count, group, ratio):
    def kernel(*refs):
        pieces, table, out = refs[:count], refs[count], refs[count + 1]
        apart, lines, lanes = pieces[0].shape
        width = out.shape[2]
        whole = jnp.concatenate(
            [piece[...].reshape(apart * lines, lanes) for piece in pieces], axis=1
        )
        done = jnp.dot(whole, table[...], precision=HIGHEST, preferred_element_type=jnp.float32)
        for block in range(ratio * group):
            out[block * apart : (block + 1) * apart] = done[
                :, block * width : (block + 1) * width
            ].reshape(apart, lines, width)

    return kernel


VMEM = pl.BlockSpec(memory_space=pltpu.VMEM)
SMEM = pl.BlockSpec(memory_space=pltpu.SMEM)
GRANT = pltpu.CompilerParams(vmem_limit_bytes=VMEM_GRANT)


def smooth(inner, outer, slab_rows, width_y, width_z):
    slabs, groups = lax.axis_size("mp"), lax.axis_size("shot")
    slab, place = lax.axis_index("mp"), lax.axis_index("shot")
    ratio = slabs // groups
    lines_y, lines_z = width_y // groups, width_z // slabs
    group = max(1, 128 // lines_y)

    table_x, spread_x = smoothing_table(slab_rows * slabs, SMOOTH_X**2)
    table_y, spread_y = smoothing_table(width_y, SMOOTH_YZ**2)
    table_z, spread_z = smoothing_table(width_z, SMOOTH_YZ**2)
    table_y = table_y * (spread_x * spread_y * spread_z)
    mix, sums = (
        lax.dynamic_index_in_dim(jnp.asarray(table), slab, 0, keepdims=False)
        for table in slab_tables(table_x, slabs)
    )
    first = lax.rem(lax.rem(slab, ratio) * groups + place, slabs)
    table_z = jnp.asarray(np.concatenate([table_z, table_z]).astype(np.float32))
    table_z = lax.dynamic_slice_in_dim(table_z, first * lines_z, width_z, 0)
    last = np.zeros((slabs, group * lines_y, ratio * group, width_y))
    for number in range(slabs):
        lines = table_y[(number % groups) * lines_y :][:lines_y]
        for part in range(group):
            last[number, part * lines_y : (part + 1) * lines_y][
                :, (number // groups) * group + part
            ] = lines
    last = last.reshape(slabs, group * lines_y, -1)
    last = last[(-np.arange(slabs)) % slabs].astype(np.float32)
    last = lax.dynamic_slice_in_dim(
        jnp.asarray(np.concatenate([last, last])), lax.rem(slabs - slab, slabs), slabs, 0
    ).reshape(slabs * group * lines_y, -1)

    block = jax.ShapeDtypeStruct((slab_rows, lines_y, width_z), jnp.float32)
    raw, planes = pl.pallas_call(
        functools.partial(mean_kernel, float(groups)),
        out_shape=(block, jax.ShapeDtypeStruct((2, lines_y, width_z), jnp.float32)),
        in_specs=[VMEM, VMEM, SMEM],
        out_specs=(VMEM, VMEM),
        compiler_params=GRANT,
        name="mean",
    )(inner, outer, sums)
    received = []
    for shift in range(1, slabs):
        upward = jnp.where(slab + shift < slabs, 1, 0)
        sent = lax.dynamic_slice_in_dim(planes, upward, 1, 0)
        ring = [(i, (i + shift) % slabs) for i in range(slabs)]
        received.append(lax.ppermute(sent, "mp", ring))
    piece = jax.ShapeDtypeStruct((slab_rows // group, lines_z, group * lines_y), jnp.float32)
    pieces = pl.pallas_call(
        make_smooth_kernel(slabs, group, lines_z),
        out_shape=(piece,) * slabs,
        in_specs=[VMEM] * slabs + [SMEM, VMEM],
        out_specs=(VMEM,) * slabs,
        scratch_shapes=[pltpu.VMEM((slab_rows, lines_y, width_z), jnp.float32)],
        compiler_params=GRANT,
        name="smooth_xz",
    )(raw, *received, mix, table_z)
    arrived = []
    for shift, sent in enumerate(pieces):
        pairs = []
        for m in range(slabs):
            for s in range(groups):
                target = ((m % ratio) * groups + s + shift) % slabs
                pairs.append((m * groups + s, target * groups + m // ratio))
        arrived.append(lax.ppermute(sent, ("mp", "shot"), pairs))
    done = pl.pallas_call(
        make_last_kernel(slabs, group, ratio),
        out_shape=jax.ShapeDtypeStruct((slab_rows * ratio, lines_z, width_y), jnp.float32),
        in_specs=[VMEM] * (slabs + 1),
        out_specs=VMEM,
        compiler_params=GRANT,
        name="smooth_y",
    )(*arrived, last)
    return raw, jnp.swapaxes(done, 1, 2)


def one_device(
    courant,
    forward_old,
    forward_now,
    adjoint_late,
    adjoint_now,
    src_cell,
    src_sign,
    wavelet,
    rec_cell,
    rec_data,
):
    shape = courant.shape
    slab_rows = shape[0]
    first_row = lax.axis_index("mp") * slab_rows
    old_fwd, now_fwd = forward_old[0], forward_now[0]
    late_adj, now_adj = adjoint_late[0], adjoint_now[0]
    tables = [jnp.asarray(table) for table in stencil_tables(shape[1], shape[2])]

    signed = (2 * src_sign[0] - 1).astype(jnp.float32)
    halo_low, halo_high = exchange(*pack_edges(now_fwd, now_adj))
    first_cell = (first_row * shape[1] * shape[2]).astype(jnp.int32).reshape(1)
    source_0, source_1, data_0, data_1 = injections(
        (src_cell[0], signed * wavelet[0, 0], signed * wavelet[0, 1]),
        (rec_cell, rec_data[0, 0], rec_data[0, 1]),
        first_cell,
        shape,
    )
    accel, next_fwd, mid_adj = slab_step(
        first_kernel, 3, now_fwd, now_adj,
        (courant, old_fwd, late_adj, source_0, data_0), tables,
    )
    accel, next_fwd, mid_adj, low_edge, high_edge = first_edges(
        halo_low, halo_high, courant, accel, next_fwd, mid_adj
    )
    halo_low, halo_high = exchange(low_edge, high_edge)
    (term,) = slab_step(
        second_kernel, 1, next_fwd, mid_adj,
        (courant, now_adj, accel, source_1, data_1), tables,
    )
    inner = sum_groups(term[REACH:-REACH])
    outer = sum_groups(second_edges(halo_low, halo_high, courant, accel, mid_adj, term))
    return smooth(inner, outer, shape[0], shape[1], shape[2])


def solution(mesh):
    return jax.shard_map(
        one_device,
        mesh=mesh,
        in_specs=(
            P(("parts", "mp"), None, None),
            P(("parts", "shot"), "mp", None, None),
            P(("parts", "shot"), "mp", None, None),
            P(("parts", "shot"), "mp", None, None),
            P(("parts", "shot"), "mp", None, None),
            P(("parts", "shot"), None),
            P(("parts", "shot"), None),
            P(("parts", "shot"), None, None),
            P("parts"),
            P(("parts", "shot"), None, None),
        ),
        out_specs=(P(("parts", "mp"), "shot", None), P(("parts", "shot"), None, "mp")),
        check_vma=False,
    )
```

profile of v0, /device:TPU:10, one launch (start us, length us, event | category | flops | bytes accessed | tf_op | source)
XLA Modules:
  0.0 161.0 jit_solution(16589582937191425706)
XLA Ops:
  0.7 2.9 %pack_edges.1 = (f32[2,4,256,128]{3,2,1,0:T(8,128)}, f32[2,4,256,128]{3,2,1,0:T(8,128)}) custom-call(f32[24,256,128]{2,1,0:T(8,128)} %bitcast.45, f32[24,256,128]{2,1,0:T(8,128)} %bitcast.46, f32[24,256,128]{2,1,0:T(8,128)} %bitcast.48, f32[24,256,128]{2,1,0:T(8,128)} %bitcast.49), custom_call_target="tpu_custom_call" | custom-call | tf_op jit(solution)/shard_map/pack_edges/pallas_call | solution.py:286
  3.6 3.5 %collective-permute-start = (f32[2,4,256,128]{3,2,1,0:T(8,128)}, f32[2,4,256,128]{3,2,1,0:T(8,128)S(1)}, u32[]{:S(2)}, u32[]{:S(2)}) collective-permute-start(f32[2,4,256,128]{3,2,1,0:T(8,128)} %get-tuple-element.22), channel_id=1, source_target_pairs={{0,4},{4,8},{8,12},{1,5},{5,9},{9,13},{2,6},{6,10},{10,14},{3,7},{... | collective-permute-start | bytes 3145736 | tf_op jit(solution)/shard_map/ppermute | solution.py:301
  7.1 2.4 %collective-permute-start.1 = (f32[2,4,256,128]{3,2,1,0:T(8,128)}, f32[2,4,256,128]{3,2,1,0:T(8,128)S(1)}, u32[]{:S(2)}, u32[]{:S(2)}) collective-permute-start(f32[2,4,256,128]{3,2,1,0:T(8,128)} %get-tuple-element.23), channel_id=1, source_target_pairs={{4,0},{8,4},{12,8},{5,1},{9,5},{13,9},{6,2},{10,6},{14,10},{7,3},{... | collective-permute-start | bytes 3145736 | tf_op jit(solution)/shard_map/ppermute | solution.py:302
  10.7 21.8 %inject.1 = (f32[6144,128]{1,0:T(8,128)}, f32[6144,128]{1,0:T(8,128)}, f32[6144,128]{1,0:T(8,128)}, f32[6144,128]{1,0:T(8,128)}) custom-call(s32[2048]{0:T(1024)} %rec_cell.1, f32[2048]{0:T(1024)} %bitcast.57, f32[2048]{0:T(1024)} %bitcast.56, s32[64]{0:T(128)} %bitcast.58, f32[64]{0:T(128)} %get-tuple-element.52.src_first, f32[64]{0:T(128)} %get-tuple-element.51.src_second, ...), custom_call_target="tpu_custom_call" | custom-call | bytes 41943040 | tf_op jit(solution)/shard_map/inject/pallas_call | solution.py:98
  32.5 16.8 %shard_map.167 = (f32[24,256,128]{2,1,0:T(8,128)}, f32[24,256,128]{2,1,0:T(8,128)}, f32[24,256,128]{2,1,0:T(8,128)}) custom-call(f32[24,256,128]{2,1,0:T(8,128)} %bitcast.47, f32[24,256,128]{2,1,0:T(8,128)} %bitcast.50, f32[24,256,128]{2,1,0:T(8,128)} %courant.7, f32[24,256,128]{2,1,0:T(8,128)} %bitcast.59, f32[24,256,128]{2,1,0:T(8,128)} %bitcast.60, ...), custom_call_target="tpu_custom_call" | custom-call | flops 8589934592 | bytes 41943040 | tf_op jit(solution)/shard_map/pallas_call | solution.py:174
  50.7 5.1 %first_edges.1 = (f32[24,256,128]{2,1,0:T(8,128)}, f32[24,256,128]{2,1,0:T(8,128)}, f32[24,256,128]{2,1,0:T(8,128)}, f32[2,4,256,128]{3,2,1,0:T(8,128)}, f32[2,4,256,128]{3,2,1,0:T(8,128)}) custom-call(f32[2,4,256,128]{3,2,1,0:T(8,128)} %copy-done, f32[2,4,256,128]{3,2,1,0:T(8,128)} %copy-done.1, ...), custom_call_target="tpu_custom_call", output_to_operand_aliasing={{0}: (3, {}), {1}: (4, {}), {2}: (5, {})} | custom-call | tf_op jit(solution)/shard_map/first_edges/pallas_call | solution.py:248
  55.8 3.8 %collective-permute-start.4 = (f32[2,4,256,128]{3,2,1,0:T(8,128)}, f32[2,4,256,128]{3,2,1,0:T(8,128)}, u32[]{:S(2)}, u32[]{:S(2)}) collective-permute-start(f32[2,4,256,128]{3,2,1,0:T(8,128)} %get-tuple-element.34), channel_id=1, source_target_pairs={{0,4},{4,8},{8,12},{1,5},{5,9},{9,13},{2,6},{6,10},{10,14},{3,7},{... | collective-permute-start | bytes 3145736 | tf_op jit(solution)/shard_map/ppermute | solution.py:301
  59.6 3.0 %collective-permute-start.5 = (f32[2,4,256,128]{3,2,1,0:T(8,128)}, f32[2,4,256,128]{3,2,1,0:T(8,128)}, u32[]{:S(2)}, u32[]{:S(2)}) collective-permute-start(f32[2,4,256,128]{3,2,1,0:T(8,128)} %get-tuple-element.35), channel_id=1, source_target_pairs={{4,0},{8,4},{12,8},{5,1},{9,5},{13,9},{6,2},{10,6},{14,10},{7,3},{... | collective-permute-start | bytes 3145736 | tf_op jit(solution)/shard_map/ppermute | solution.py:302
  62.7 15.4 %shard_map.168.term = f32[24,256,128]{2,1,0:T(8,128)} custom-call(f32[24,256,128]{2,1,0:T(8,128)} %get-tuple-element.29.f_now, f32[24,256,128]{2,1,0:T(8,128)} %get-tuple-element.30.a_now.a_mid, f32[24,256,128]{2,1,0:T(8,128)} %courant.7, f32[24,256,128]{2,1,0:T(8,128)} %bitcast.51, f32[24,256,128]{2,1,0:T(8,128)} %get-tuple-element.31.accel, ...), custom_call_target="tpu_custom_call" | custom-call | flops 8589934592 | bytes 41943040 | tf_op jit(solution)/shard_map/pallas_call | solution.py:174
  82.3 4.2 %collective-permute-done.5.halo_high = f32[2,4,256,128]{3,2,1,0:T(8,128)} collective-permute-done((f32[2,4,256,128]{3,2,1,0:T(8,128)}, f32[2,4,256,128]{3,2,1,0:T(8,128)}, u32[]{:S(2)}, u32[]{:S(2)}) %collective-permute-start.5) | collective-permute-done | bytes 1048608 | tf_op jit(solution)/shard_map/ppermute | solution.py:302
  86.5 3.8 %second_edges.1 = f32[8,256,128]{2,1,0:T(8,128)} custom-call(f32[2,4,256,128]{3,2,1,0:T(8,128)} %collective-permute-done.4.halo_low, f32[2,4,256,128]{3,2,1,0:T(8,128)} %collective-permute-done.5.halo_high, f32[24,256,128]{2,1,0:T(8,128)} %courant.7, f32[24,256,128]{2,1,0:T(8,128)} %get-tuple-element.31.accel, ...), custom_call_target="tpu_custom_call" | custom-call | tf_op jit(solution)/shard_map/second_edges/pallas_call | solution.py:263
  100.9 8.9 %collective-permute-done.3 = f32[16,1,64,128]{3,2,0,1:T(8,128)S(1)} collective-permute-done((f32[16,1,64,128]{3,2,0,1:T(8,128)S(1)}, f32[16,1,64,128]{3,2,0,1:T(8,128)S(1)}, u32[]{:S(2)}, u32[]{:S(2)}) %collective-permute-start.3) | collective-permute-done | bytes 524320 | tf_op jit(solution)/shard_map/ppermute | solution.py:317
  110.6 4.3 %collective-permute-done.7 = f32[8,1,64,128]{3,2,0,1:T(8,128)S(1)} collective-permute-done((f32[8,1,64,128]{3,2,0,1:T(8,128)S(1)}, f32[8,1,64,128]{3,2,0,1:T(8,128)S(1)}, u32[]{:S(2)}, u32[]{:S(2)}) %collective-permute-start.7) | collective-permute-done | bytes 262176 | tf_op jit(solution)/shard_map/ppermute | solution.py:317
  115.7 2.1 %mean.1 = (f32[24,64,128]{2,1,0:T(8,128)}, f32[2,64,128]{2,1,0:T(8,128)}) custom-call(f32[16,64,128]{2,1,0:T(8,128)} %add_bitcast_fusion.inner, f32[8,64,128]{2,1,0:T(8,128)} %add_bitcast_fusion.1.outer, f32[2,24]{1,0:T(2,128)} %fusion.2.sums), custom_call_target="tpu_custom_call" | custom-call | tf_op jit(solution)/shard_map/mean/pallas_call | solution.py:450
  120.7 2.6 %collective-permute-start.9 = (f32[1,64,128]{2,1,0:T(8,128)S(1)}, f32[1,64,128]{2,1,0:T(8,128)S(1)}, u32[]{:S(2)}, u32[]{:S(2)}) collective-permute-start(f32[1,64,128]{2,1,0:T(8,128)S(1)} %get-tuple-element.47), channel_id=1, source_target_pairs={{0,8},{4,12},{8,0},{12,4},{1,9},{5,13},{9,1},{13,5},{2,10},{6,14},... | collective-permute-start | bytes 98312 | tf_op jit(solution)/shard_map/ppermute | solution.py:463
  126.1 5.3 %smooth_xz.1 = (f32[12,32,128]{2,1,0:T(8,128)}, f32[12,32,128]{2,1,0:T(8,128)}, f32[12,32,128]{2,1,0:T(8,128)}, f32[12,32,128]{2,1,0:T(8,128)}) custom-call(f32[24,64,128]{2,1,0:T(8,128)} %get-tuple-element.20.raw, f32[1,64,128]{2,1,0:T(8,128)} %copy-done.10, f32[1,64,128]{2,1,0:T(8,128)} %copy-done.11, f32[1,64,128]{2,1,0:T(8,128)} %copy-done.9, ...), custom_call_target="tpu_custom_call" | custom-call | tf_op jit(solution)/shard_map/smooth_xz/pallas_call | solution.py:465
  131.4 1.9 %collective-permute-start.11 = (f32[12,32,128]{2,1,0:T(8,128)}, f32[12,32,128]{2,1,0:T(8,128)S(1)}, u32[]{:S(2)}, u32[]{:S(2)}) collective-permute-start(f32[12,32,128]{2,1,0:T(8,128)} %get-tuple-element.38), channel_id=1, source_target_pairs={{0,0},{1,4},{2,8},{3,12},{4,1},{5,5},{6,9},{7,13},{8,2},{9,6},{10,... | collective-permute-start | bytes 589832 | tf_op jit(solution)/shard_map/ppermute | solution.py:481
  133.3 1.7 %collective-permute-start.12 = (f32[12,32,128]{2,1,0:T(8,128)}, f32[12,32,128]{2,1,0:T(8,128)S(1)}, u32[]{:S(2)}, u32[]{:S(2)}) collective-permute-start(f32[12,32,128]{2,1,0:T(8,128)} %get-tuple-element.39), channel_id=1, source_target_pairs={{0,4},{1,8},{2,12},{3,0},{4,5},{5,9},{6,13},{7,1},{8,6},{9,10},{10... | collective-permute-start | bytes 589832 | tf_op jit(solution)/shard_map/ppermute | solution.py:481
  135.1 2.9 %collective-permute-start.13 = (f32[12,32,128]{2,1,0:T(8,128)}, f32[12,32,128]{2,1,0:T(8,128)S(1)}, u32[]{:S(2)}, u32[]{:S(2)}) collective-permute-start(f32[12,32,128]{2,1,0:T(8,128)} %get-tuple-element.40), channel_id=1, source_target_pairs={{0,8},{1,12},{2,0},{3,4},{4,9},{5,13},{6,1},{7,5},{8,10},{9,14},{1... | collective-permute-start | bytes 589832 | tf_op jit(solution)/shard_map/ppermute | solution.py:481
  138.9 2.3 %constant_dynamic-slice_fusion = f32[4,128,512]{2,1,0:T(8,128)} fusion(f32[8,128,512]{2,1,0:T(8,128)} %constant.132.clone, s32[]{:T(128)S(6)} %select_n.79), kind=kLoop, calls=%fused_computation.9 | loop fusion | bytes 2097156 | tf_op jit(solution)/shard_map/dynamic_slice | solution.py:445
  141.2 7.8 %collective-permute-done.11.refs_0_ = f32[12,32,128]{2,1,0:T(8,128)S(1)} collective-permute-done((f32[12,32,128]{2,1,0:T(8,128)}, f32[12,32,128]{2,1,0:T(8,128)S(1)}, u32[]{:S(2)}, u32[]{:S(2)}) %collective-permute-start.11) | collective-permute-done | bytes 196640 | tf_op jit(solution)/shard_map/ppermute | solution.py:481
  149.0 4.3 %collective-permute-done.12.refs_1_ = f32[12,32,128]{2,1,0:T(8,128)S(1)} collective-permute-done((f32[12,32,128]{2,1,0:T(8,128)}, f32[12,32,128]{2,1,0:T(8,128)S(1)}, u32[]{:S(2)}, u32[]{:S(2)}) %collective-permute-start.12) | collective-permute-done | bytes 196640 | tf_op jit(solution)/shard_map/ppermute | solution.py:481
  154.8 1.6 %collective-permute-done.14.refs_3_ = f32[12,32,128]{2,1,0:T(8,128)S(1)} collective-permute-done((f32[12,32,128]{2,1,0:T(8,128)}, f32[12,32,128]{2,1,0:T(8,128)S(1)}, u32[]{:S(2)}, u32[]{:S(2)}) %collective-permute-start.14) | collective-permute-done | bytes 196640 | tf_op jit(solution)/shard_map/ppermute | solution.py:481
  157.1 3.9 %smooth_y.1 = f32[24,32,256]{2,1,0:T(8,128)} custom-call(f32[12,32,128]{2,1,0:T(8,128)} %copy-done.4, f32[12,32,128]{2,1,0:T(8,128)} %copy-done.5, f32[12,32,128]{2,1,0:T(8,128)} %copy-done.6, f32[12,32,128]{2,1,0:T(8,128)} %copy-done.7, f32[512,512]{1,0:T(8,128)} %bitcast.53), custom_call_target="tpu_custom_call" | custom-call | tf_op jit(solution)/shard_map/smooth_y/pallas_call | solution.py:482
  (64 shorter events, 27.8 us)
Async XLA Ops:
  0.6 8.9 %copy-start.12 = (f32[1,2,2048]{2,1,0:T(2,128)S(1)}, f32[1,2,2048]{2,1,0:T(2,128)}, u32[]{:S(2)}) copy-start(f32[1,2,2048]{2,1,0:T(2,128)} %param.25) | copy-start | bytes 49156
  0.6 9.5 %copy-start.13 = (f32[1,2,64]{2,1,0:T(2,128)S(1)}, f32[1,2,64]{2,1,0:T(2,128)}, u32[]{:S(2)}) copy-start(f32[1,2,64]{2,1,0:T(2,128)} %param.23) | copy-start | bytes 1540
  0.7 9.5 %copy-start.14 = (s32[1,64]{1,0:T(1,128)S(1)}, s32[1,64]{1,0:T(1,128)}, u32[]{:S(2)}) copy-start(s32[1,64]{1,0:T(1,128)} %param.22) | copy-start | bytes 772
  3.6 45.7 %collective-permute-start = (f32[2,4,256,128]{3,2,1,0:T(8,128)}, f32[2,4,256,128]{3,2,1,0:T(8,128)S(1)}, u32[]{:S(2)}, u32[]{:S(2)}) collective-permute-start(f32[2,4,256,128]{3,2,1,0:T(8,128)} %get-tuple-element.22), channel_id=1, source_target_pairs={{0,4},{4,8},{8,12},{1,5},{5,9},{9,13},{2,6},{6,10},{10,14},{3,7},{... | collective-permute-start | bytes 3145736 | tf_op jit(solution)/shard_map/ppermute | solution.py:301
  7.1 42.2 %collective-permute-start.1 = (f32[2,4,256,128]{3,2,1,0:T(8,128)}, f32[2,4,256,128]{3,2,1,0:T(8,128)S(1)}, u32[]{:S(2)}, u32[]{:S(2)}) collective-permute-start(f32[2,4,256,128]{3,2,1,0:T(8,128)} %get-tuple-element.23), channel_id=1, source_target_pairs={{4,0},{8,4},{12,8},{5,1},{9,5},{13,9},{6,2},{10,6},{14,10},{7,3},{... | collective-permute-start | bytes 3145736 | tf_op jit(solution)/shard_map/ppermute | solution.py:302
  49.3 1.4 copy-start.1
  55.8 26.5 %collective-permute-start.4 = (f32[2,4,256,128]{3,2,1,0:T(8,128)}, f32[2,4,256,128]{3,2,1,0:T(8,128)}, u32[]{:S(2)}, u32[]{:S(2)}) collective-permute-start(f32[2,4,256,128]{3,2,1,0:T(8,128)} %get-tuple-element.34), channel_id=1, source_target_pairs={{0,4},{4,8},{8,12},{1,5},{5,9},{9,13},{2,6},{6,10},{10,14},{3,7},{... | collective-permute-start | bytes 3145736 | tf_op jit(solution)/shard_map/ppermute | solution.py:301
  59.6 26.9 %collective-permute-start.5 = (f32[2,4,256,128]{3,2,1,0:T(8,128)}, f32[2,4,256,128]{3,2,1,0:T(8,128)}, u32[]{:S(2)}, u32[]{:S(2)}) collective-permute-start(f32[2,4,256,128]{3,2,1,0:T(8,128)} %get-tuple-element.35), channel_id=1, source_target_pairs={{4,0},{8,4},{12,8},{5,1},{9,5},{13,9},{6,2},{10,6},{14,10},{7,3},{... | collective-permute-start | bytes 3145736 | tf_op jit(solution)/shard_map/ppermute | solution.py:302
  78.1 1.6 slice-start
  81.0 11.6 %collective-permute-start.2 = (f32[16,2,64,128]{3,2,0,1:T(8,128)}, f32[16,2,64,128]{3,2,0,1:T(8,128)S(1)}, u32[]{:S(2)}, u32[]{:S(2)}) collective-permute-start(f32[16,2,64,128]{3,2,0,1:T(8,128)} %bitcast.43), channel_id=1, source_target_pairs={{0,1},{1,0},{2,3},{3,2},{4,5},{5,4},{6,7},{7,6},{8,9},{9,8},{10,11... | collective-permute-start | bytes 3145736 | tf_op jit(solution)/shard_map/ppermute | solution.py:317
  91.7 4.1 %copy-start.8 = (f32[256,128]{1,0:T(8,128)S(1)}, f32[256,128]{1,0:T(8,128)}, u32[]{:S(2)}) copy-start(f32[256,128]{1,0:T(8,128)} %constant.131.clone) | copy-start | bytes 393220
  92.5 3.9 %collective-permute-start.6 = (f32[8,2,64,128]{3,2,0,1:T(8,128)}, f32[8,2,64,128]{3,2,0,1:T(8,128)S(1)}, u32[]{:S(2)}, u32[]{:S(2)}) collective-permute-start(f32[8,2,64,128]{3,2,0,1:T(8,128)} %bitcast.44), channel_id=1, source_target_pairs={{0,1},{1,0},{2,3},{3,2},{4,5},{5,4},{6,7},{7,6},{8,9},{9,8},{10,11... | collective-permute-start | bytes 1572872 | tf_op jit(solution)/shard_map/ppermute | solution.py:317
  94.9 14.9 %collective-permute-start.3 = (f32[16,1,64,128]{3,2,0,1:T(8,128)S(1)}, f32[16,1,64,128]{3,2,0,1:T(8,128)S(1)}, u32[]{:S(2)}, u32[]{:S(2)}) collective-permute-start(f32[16,1,64,128]{3,2,0,1:T(8,128)S(1)} %constant_dynamic-slice_fusion.9), channel_id=1, source_target_pairs={{0,2},{1,3},{2,0},{3,1},{4,6},{5,7},{6,4},{7,5},{8,10},{9,11},{10,... | collective-permute-start | bytes 1572872 | tf_op jit(solution)/shard_map/ppermute | solution.py:317
  98.4 16.6 %collective-permute-start.7 = (f32[8,1,64,128]{3,2,0,1:T(8,128)S(1)}, f32[8,1,64,128]{3,2,0,1:T(8,128)S(1)}, u32[]{:S(2)}, u32[]{:S(2)}) collective-permute-start(f32[8,1,64,128]{3,2,0,1:T(8,128)S(1)} %constant_dynamic-slice_fusion.6), channel_id=1, source_target_pairs={{0,2},{1,3},{2,0},{3,1},{4,6},{5,7},{6,4},{7,5},{8,10},{9,11},{10,... | collective-permute-start | bytes 786440 | tf_op jit(solution)/shard_map/ppermute | solution.py:317
  118.6 5.9 %collective-permute-start.10 = (f32[1,64,128]{2,1,0:T(8,128)S(1)}, f32[1,64,128]{2,1,0:T(8,128)S(1)}, u32[]{:S(2)}, u32[]{:S(2)}) collective-permute-start(f32[1,64,128]{2,1,0:T(8,128)S(1)} %get-tuple-element.46), channel_id=1, source_target_pairs={{0,12},{4,0},{8,4},{12,8},{1,13},{5,1},{9,5},{13,9},{2,14},{6,2},{... | collective-permute-start | bytes 98312 | tf_op jit(solution)/shard_map/ppermute | solution.py:463
  119.2 5.4 %collective-permute-start.8 = (f32[1,64,128]{2,1,0:T(8,128)S(1)}, f32[1,64,128]{2,1,0:T(8,128)S(1)}, u32[]{:S(2)}, u32[]{:S(2)}) collective-permute-start(f32[1,64,128]{2,1,0:T(8,128)S(1)} %get-tuple-element.48), channel_id=1, source_target_pairs={{0,4},{4,8},{8,12},{12,0},{1,5},{5,9},{9,13},{13,1},{2,6},{6,10},{... | collective-permute-start | bytes 98312 | tf_op jit(solution)/shard_map/ppermute | solution.py:463
  120.7 4.8 %collective-permute-start.9 = (f32[1,64,128]{2,1,0:T(8,128)S(1)}, f32[1,64,128]{2,1,0:T(8,128)S(1)}, u32[]{:S(2)}, u32[]{:S(2)}) collective-permute-start(f32[1,64,128]{2,1,0:T(8,128)S(1)} %get-tuple-element.47), channel_id=1, source_target_pairs={{0,8},{4,12},{8,0},{12,4},{1,9},{5,13},{9,1},{13,5},{2,10},{6,14},... | collective-permute-start | bytes 98312 | tf_op jit(solution)/shard_map/ppermute | solution.py:463
  131.4 17.6 %collective-permute-start.11 = (f32[12,32,128]{2,1,0:T(8,128)}, f32[12,32,128]{2,1,0:T(8,128)S(1)}, u32[]{:S(2)}, u32[]{:S(2)}) collective-permute-start(f32[12,32,128]{2,1,0:T(8,128)} %get-tuple-element.38), channel_id=1, source_target_pairs={{0,0},{1,4},{2,8},{3,12},{4,1},{5,5},{6,9},{7,13},{8,2},{9,6},{10,... | collective-permute-start | bytes 589832 | tf_op jit(solution)/shard_map/ppermute | solution.py:481
  133.3 20.0 %collective-permute-start.12 = (f32[12,32,128]{2,1,0:T(8,128)}, f32[12,32,128]{2,1,0:T(8,128)S(1)}, u32[]{:S(2)}, u32[]{:S(2)}) collective-permute-start(f32[12,32,128]{2,1,0:T(8,128)} %get-tuple-element.39), channel_id=1, source_target_pairs={{0,4},{1,8},{2,12},{3,0},{4,5},{5,9},{6,13},{7,1},{8,6},{9,10},{10... | collective-permute-start | bytes 589832 | tf_op jit(solution)/shard_map/ppermute | solution.py:481
  135.1 19.8 %collective-permute-start.13 = (f32[12,32,128]{2,1,0:T(8,128)}, f32[12,32,128]{2,1,0:T(8,128)S(1)}, u32[]{:S(2)}, u32[]{:S(2)}) collective-permute-start(f32[12,32,128]{2,1,0:T(8,128)} %get-tuple-element.40), channel_id=1, source_target_pairs={{0,8},{1,12},{2,0},{3,4},{4,9},{5,13},{6,1},{7,5},{8,10},{9,14},{1... | collective-permute-start | bytes 589832 | tf_op jit(solution)/shard_map/ppermute | solution.py:481
  138.0 18.4 %collective-permute-start.14 = (f32[12,32,128]{2,1,0:T(8,128)}, f32[12,32,128]{2,1,0:T(8,128)S(1)}, u32[]{:S(2)}, u32[]{:S(2)}) collective-permute-start(f32[12,32,128]{2,1,0:T(8,128)} %get-tuple-element.41), channel_id=1, source_target_pairs={{0,12},{1,0},{2,4},{3,8},{4,13},{5,1},{6,5},{7,9},{8,14},{9,2},{10... | collective-permute-start | bytes 589832 | tf_op jit(solution)/shard_map/ppermute | solution.py:481
  149.0 7.5 %copy-start.4 = (f32[12,32,128]{2,1,0:T(8,128)}, f32[12,32,128]{2,1,0:T(8,128)S(1)}, u32[]{:S(2)}) copy-start(f32[12,32,128]{2,1,0:T(8,128)S(1)} %collective-permute-done.11.refs_0_) | copy-start | bytes 589828
  153.3 3.2 %copy-start.5 = (f32[12,32,128]{2,1,0:T(8,128)}, f32[12,32,128]{2,1,0:T(8,128)S(1)}, u32[]{:S(2)}) copy-start(f32[12,32,128]{2,1,0:T(8,128)S(1)} %collective-permute-done.12.refs_1_) | copy-start | bytes 589828
  154.8 1.6 %copy-start.6 = (f32[12,32,128]{2,1,0:T(8,128)}, f32[12,32,128]{2,1,0:T(8,128)S(1)}, u32[]{:S(2)}) copy-start(f32[12,32,128]{2,1,0:T(8,128)S(1)} %collective-permute-done.13.refs_2_) | copy-start | bytes 589828
  (7 other events, 6.0 us)
where the time goes:
time: 162 us; the launch traced here: 161 us
  Pallas kernels  77.2 us (48%)
  waiting for transfers between devices  34.9 us (22%)
  starting transfers between devices  27 us (17%)
  local copies, waits for them, and re-layouts  16.5 us (10%)
  other arithmetic  4.61 us (3%)
    pallas_call x2, Pallas kernels, slab_step(): pl.pallas_call(kernel, grid=(blocks,), out_shape=(shape,) * outs, in_spec...  32.2 us
    pallas_call x1, Pallas kernels, injections(): pl.pallas_call(scatter_kernel, out_shape=(flat,) * 4, in_specs=[pl.BlockS...  21.8 us
    ppermute x4, waiting for transfers between devices, smooth(): arrived.append(lax.ppermute(sent, ('mp', 'shot'), pairs))  15.2 us
    ppermute x4, waiting for transfers between devices, sum_groups(): sent = lax.ppermute(other, 'shot', [(i, i ^ bit) for i in range(count)])  13.2 us
    ppermute x4, starting transfers between devices, smooth(): arrived.append(lax.ppermute(sent, ('mp', 'shot'), pairs))  7.51 us
    ppermute x2, starting transfers between devices, exchange(): from_low = lax.ppermute(high_edge, 'mp', upward)  7.29 us
    unnamed x32, local copies, waits for them, and re-layouts  6.34 us
    ppermute x2, starting transfers between devices, exchange(): from_high = lax.ppermute(low_edge, 'mp', downward)  5.45 us
  transfers between devices with their start and end apart: 15, of which 9 were waited for; matrix products, arithmetic and copies ran while one was open for 8% of the time, Pallas kernels for 36%

commit v1 on v0

--- a/solution.py
+++ b/solution.py
@@ -28,69 +28,71 @@
     return table, 1.0 / math.sqrt(np.mean(resp * resp))
 
 
-def stencil_table(length, center):
-    table = np.eye(length) * center
-    for offset, weight in enumerate(COEFS):
-        reach = offset + 1
-        if reach < length:
-            table += weight * (np.eye(length, k=reach) + np.eye(length, k=-reach))
-    return table
-
-
-def split_table(table):
-    high = jnp.asarray(table, jnp.float32).astype(jnp.bfloat16)
-    rest = table - np.asarray(high.astype(jnp.float32), np.float64)
-    return np.asarray(high), np.asarray(jnp.asarray(rest, jnp.float32).astype(jnp.bfloat16))
+SCALE = 5040.0
+WHOLE = tuple(float(round(SCALE * weight)) for weight in COEFS)
+MIDDLE = 3.0 * float(round(SCALE * CENTER))
 
 
 def stencil_tables(width_y, width_z):
-    with jax.ensure_compile_time_eval():
-        y_high, y_low = split_table(stencil_table(width_y, 3.0 * CENTER))
-        z_high, z_low = split_table(np.kron(np.eye(2), stencil_table(width_z, 0.0)))
-    table_y = np.concatenate([y_high, y_high, y_low], axis=1)
-    table_z = np.concatenate([z_high, z_high, z_low], axis=0)
-    return table_y, table_z
+    def bands(length):
+        return sum(
+            weight * (np.eye(length, k=offset + 1) + np.eye(length, k=-offset - 1))
+            for offset, weight in enumerate(WHOLE)
+        )
+
+    band_y = bands(width_y)
+    band_z = np.kron(np.eye(2), bands(width_z))
+    return (
+        jnp.asarray(np.concatenate([band_y, band_y], axis=1), jnp.bfloat16),
+        jnp.asarray(np.concatenate([band_z, band_z], axis=0), jnp.bfloat16),
+    )
 
 
 def scatter_kernel(
-    rec_cell, rec_first, rec_second, src_cell, src_first, src_second, base, *outs
+    rec_row, rec_lane, rec_first, rec_second, src_row, src_lane, src_first, src_second, *outs
 ):
-    *outs, rec_list, src_list = outs
     source_0, source_1, data_0, data_1 = outs
-    rows, width = source_0.shape
     zero = jnp.zeros(source_0.shape, jnp.float32)
     for out in outs:
         out[...] = zero
-    lanes = lax.broadcasted_iota(jnp.int32, (1, width), 1)
-    first_cell = base[0]
-
-    def add_all(cells, first, second, found, out_first, out_second):
-        count = cells.shape[0]
-        unroll = math.gcd(count, 16)
-
-        def keep(step, kept):
-            for extra in range(unroll):
-                item = step * unroll + extra
-                local = cells[item] - first_cell
-                found[kept] = item
-                kept += jnp.where((local >= 0) & (local < rows * width), 1, 0)
-            return kept
-
-        kept = lax.fori_loop(0, count // unroll, keep, 0)
-
-        def add_one(step, carry):
-            item = found[step]
-            local = cells[item] - first_cell
-            row = local // width
-            hit = lanes == local - row * width
-            out_first[pl.ds(row, 1), :] += jnp.where(hit, first[item], 0.0)
-            out_second[pl.ds(row, 1), :] += jnp.where(hit, second[item], 0.0)
+    lanes = lax.broadcasted_iota(jnp.int32, (1, source_0.shape[1]), 1)
+
+    def add_all(rows, columns, first, second, targets):
+        count = rows.shape[0]
+        group = math.gcd(count, 4)
+
+        def some(step, carry):
+            items = [step * group + extra for extra in range(group)]
+            places = [rows[item] for item in items]
+            hits = [lanes == columns[item] for item in items]
+            for values, out in zip((first, second), targets):
+                added = [jnp.where(hit, values[item], 0.0) for hit, item in zip(hits, items)]
+                sums = []
+                for late in range(group):
+                    total = added[late]
+                    for early in range(late):
+                        total += jnp.where(places[early] == places[late], added[early], 0.0)
+                    sums.append(out[pl.ds(places[late], 1), :] + total)
+                for place, total in zip(places, sums):
+                    out[pl.ds(place, 1), :] = total
             return carry
 
-        lax.fori_loop(0, kept, add_one, 0)
-
-    add_all(rec_cell, rec_first, rec_second, rec_list, data_0, data_1)
-    add_all(src_cell, src_first, src_second, src_list, source_0, source_1)
+        lax.fori_loop(0, count // group, some, 0)
+
+    add_all(rec_row, rec_lane, rec_first, rec_second, (data_0, data_1))
+    add_all(src_row, src_lane, src_first, src_second, (source_0, source_1))
+
+
+def localize(cells, first, second, first_cell, shape):
+    local = cells - first_cell
+    valid = (local >= 0) & (local < shape[0] * shape[1] * shape[2])
+    local = jnp.where(valid, local, 0)
+    return (
+        local // shape[2],
+        local % shape[2],
+        jnp.where(valid, first, 0.0),
+        jnp.where(valid, second, 0.0),
+    )
 
 
 def injections(src, rec, first_cell, shape):
@@ -98,52 +100,73 @@
     outs = pl.pallas_call(
         scatter_kernel,
         out_shape=(flat,) * 4,
-        in_specs=[pl.BlockSpec(memory_space=pltpu.SMEM)] * 7,
+        in_specs=[pl.BlockSpec(memory_space=pltpu.SMEM)] * 8,
         out_specs=(pl.BlockSpec(memory_space=pltpu.VMEM),) * 4,
-        scratch_shapes=[
-            pltpu.SMEM((rec[0].shape[0] + 16,), jnp.int32),
-            pltpu.SMEM((src[0].shape[0] + 16,), jnp.int32),
-        ],
         compiler_params=pltpu.CompilerParams(vmem_limit_bytes=VMEM_GRANT),
         cost_estimate=pl.CostEstimate(flops=0, bytes_accessed=40 * 2**20, transcendentals=0),
         name="inject",
-    )(*rec, *src, first_cell)
+    )(*localize(*rec, first_cell, shape), *localize(*src, first_cell, shape))
     return [out.reshape(shape) for out in outs]
 
 
+def load_fields(sources, fields, sems):
+    step, blocks = pl.program_id(0), pl.num_programs(0)
+    count = sources[0].shape[0] // REACH
+
+    def copy(side, block):
+        return pltpu.make_async_copy(
+            sources[side].at[pl.ds(block * REACH, REACH)],
+            fields[side].at[pl.ds((block + 1) * REACH, REACH)],
+            sems.at[side, block],
+        )
+
+    @pl.when(step == 0)
+    def _():
+        for block in range(count):
+            for side in range(2):
+                copy(side, block).start()
+        for field in fields:
+            zero = jnp.zeros((REACH,) + field.shape[1:], jnp.float32)
+            field[:REACH] = zero
+            field[(count + 1) * REACH :] = zero
+        for side in range(2):
+            copy(side, 0).wait()
+
+    @pl.when(step + 1 < blocks)
+    def _():
+        for side in range(2):
+            copy(side, step + 1).wait()
+
+
 def slab_laplace(place, fields, table_y, table_z):
-    count = fields[0].shape[0]
-    both = jnp.concatenate([field[place] for field in fields], axis=1)
+    planes = [field[place] for field in fields]
+    both = jnp.concatenate(planes, axis=1)
     high = both.astype(jnp.bfloat16)
     low = (both - high.astype(jnp.float32)).astype(jnp.bfloat16)
     total = jnp.dot(
-        table_y[...],
-        jnp.concatenate([high, low, high], axis=0),
-        preferred_element_type=jnp.float32,
+        table_y[...], jnp.concatenate([high, low], axis=0), preferred_element_type=jnp.float32
     ) + jnp.dot(
-        jnp.concatenate([high, low, high], axis=1),
-        table_z[...],
-        preferred_element_type=jnp.float32,
+        jnp.concatenate([high, low], axis=1), table_z[...], preferred_element_type=jnp.float32
     )
     width = fields[0].shape[2]
-    laps = [total[:, side * width : (side + 1) * width] for side in range(2)]
-    for offset, weight in enumerate(COEFS):
-        for shift in (offset + 1, -(offset + 1)):
-            other = place + shift
-            inside = (other >= 0) & (other < count)
-            factor = jnp.where(inside, weight, 0.0).astype(jnp.float32)
-            other = jnp.clip(other, 0, count - 1)
-            laps = [lap + factor * field[other] for lap, field in zip(laps, fields)]
+    laps = []
+    for side, field in enumerate(fields):
+        lap = total[:, side * width : (side + 1) * width] + MIDDLE * planes[side]
+        for offset, weight in enumerate(WHOLE):
+            lap += weight * (field[place + offset + 1] + field[place - offset - 1])
+        laps.append(lap)
     return laps
 
 
 def first_kernel(
-    f_now, a_now, courant, f_old, a_late, source, data, table_y, table_z, accel, f_next, a_mid
+    f_all, a_all, courant, f_old, a_late, source, data, table_y, table_z,
+    accel, f_next, a_mid, f_now, a_now, sems,
 ):
+    load_fields((f_all, a_all), (f_now, a_now), sems)
     for row in range(REACH):
-        place = pl.program_id(0) * REACH + row
+        place = (pl.program_id(0) + 1) * REACH + row
         lap_f, lap_a = slab_laplace(place, (f_now, a_now), table_y, table_z)
-        here = courant[row]
+        here = courant[row] * (1.0 / SCALE)
         accel_row = here * lap_f + source[row]
         accel[row] = accel_row
         f_next[row] = (2.0 * f_now[place] - f_old[row]) + accel_row
@@ -151,12 +174,14 @@
 
 
 def second_kernel(
-    f_now, a_now, courant, a_old, accel, source, data, table_y, table_z, term
+    f_all, a_all, courant, a_old, accel, source, data, table_y, table_z, term,
+    f_now, a_now, sems,
 ):
+    load_fields((f_all, a_all), (f_now, a_now), sems)
     for row in range(REACH):
-        place = pl.program_id(0) * REACH + row
+        place = (pl.program_id(0) + 1) * REACH + row
         lap_f, lap_a = slab_laplace(place, (f_now, a_now), table_y, table_z)
-        here = courant[row]
+        here = courant[row] * (1.0 / SCALE)
         accel_second = here * lap_f + source[row]
         a_row = a_now[place]
         a_first = (2.0 * a_row - a_old[row]) + (here * lap_a + data[row])
@@ -166,17 +191,17 @@
 def slab_step(kernel, outs, field_f, field_a, others, tables):
     rows, width_y, width_z = field_f.shape
     blocks = rows // REACH
-    block = (REACH, width_y, width_z)
-    here = pl.BlockSpec(block, lambda i: (i, 0, 0))
-    field = pl.BlockSpec(field_f.shape, lambda i: (0, 0, 0))
+    here = pl.BlockSpec((REACH, width_y, width_z), lambda i: (i, 0, 0))
     whole = [pl.BlockSpec(table.shape, lambda i: (0, 0)) for table in tables]
     shape = jax.ShapeDtypeStruct(field_f.shape, jnp.float32)
+    padded = pltpu.VMEM((rows + 2 * REACH, width_y, width_z), jnp.float32)
     return pl.pallas_call(
         kernel,
         grid=(blocks,),
         out_shape=(shape,) * outs,
-        in_specs=[field] * 2 + [here] * len(others) + whole,
+        in_specs=[pl.BlockSpec(memory_space=pl.ANY)] * 2 + [here] * len(others) + whole,
         out_specs=(here,) * outs,
+        scratch_shapes=[padded, padded, pltpu.SemaphoreType.DMA((2, blocks))],
         compiler_params=pltpu.CompilerParams(
             dimension_semantics=("arbitrary",), vmem_limit_bytes=VMEM_GRANT
         ),
@@ -238,7 +263,7 @@
     return both, edge, side
 
 
-EDGE_PARAMS = dict(dimension_semantics=("arbitrary",), vmem_limit_bytes=VMEM_GRANT)
+EDGE_PARAMS = dict(dimension_semantics=("arbitrary",), vmem_limit_bytes=40 * 2**20)
 
 
 def first_edges(low, high, courant, accel, f_next, a_mid):
@@ -393,18 +418,28 @@
     return kernel
 
 
-def make_last_kernel(count, group, ratio):
+def make_last_kernel(count, group, groups):
     def kernel(*refs):
-        pieces, table, out = refs[:count], refs[count], refs[count + 1]
+        pieces, table, out, spread = refs[:count], refs[count], refs[count + 1], refs[count + 2]
         apart, lines, lanes = pieces[0].shape
         width = out.shape[2]
+        block = width // groups
+        slab = lax.axis_index("mp")
+        spread[...] = jnp.zeros(spread.shape, jnp.float32)
+        for shift in range(count):
+            number = lax.rem(slab + (count - shift), count)
+            rows = table[pl.ds(pl.multiple_of(lax.rem(number, groups) * block, block), block), :]
+            for part in range(group):
+                column = (lax.div(number, groups) * group + part) * width
+                top = shift * lanes + part * block
+                spread[top : top + block, pl.ds(pl.multiple_of(column, width), width)] = rows
         whole = jnp.concatenate(
             [piece[...].reshape(apart * lines, lanes) for piece in pieces], axis=1
         )
-        done = jnp.dot(whole, table[...], precision=HIGHEST, preferred_element_type=jnp.float32)
-        for block in range(ratio * group):
-            out[block * apart : (block + 1) * apart] = done[
-                :, block * width : (block + 1) * width
+        done = jnp.dot(whole, spread[...], precision=HIGHEST, preferred_element_type=jnp.float32)
+        for place in range(count // groups * group):
+            out[place * apart : (place + 1) * apart] = done[
+                :, place * width : (place + 1) * width
             ].reshape(apart, lines, width)
 
     return kernel
@@ -412,7 +447,7 @@
 
 VMEM = pl.BlockSpec(memory_space=pltpu.VMEM)
 SMEM = pl.BlockSpec(memory_space=pltpu.SMEM)
-GRANT = pltpu.CompilerParams(vmem_limit_bytes=VMEM_GRANT)
+GRANT = pltpu.CompilerParams(vmem_limit_bytes=40 * 2**20)
 
 
 def smooth(inner, outer, slab_rows, width_y, width_z):
@@ -433,19 +468,7 @@
     first = lax.rem(lax.rem(slab, ratio) * groups + place, slabs)
     table_z = jnp.asarray(np.concatenate([table_z, table_z]).astype(np.float32))
     table_z = lax.dynamic_slice_in_dim(table_z, first * lines_z, width_z, 0)
-    last = np.zeros((slabs, group * lines_y, ratio * group, width_y))
-    for number in range(slabs):
-        lines = table_y[(number % groups) * lines_y :][:lines_y]
-        for part in range(group):
-            last[number, part * lines_y : (part + 1) * lines_y][
-                :, (number // groups) * group + part
-            ] = lines
-    last = last.reshape(slabs, group * lines_y, -1)
-    last = last[(-np.arange(slabs)) % slabs].astype(np.float32)
-    last = lax.dynamic_slice_in_dim(
-        jnp.asarray(np.concatenate([last, last])), lax.rem(slabs - slab, slabs), slabs, 0
-    ).reshape(slabs * group * lines_y, -1)
-
+    table_y = jnp.asarray(table_y, jnp.float32)
     block = jax.ShapeDtypeStruct((slab_rows, lines_y, width_z), jnp.float32)
     raw, planes = pl.pallas_call(
         functools.partial(mean_kernel, float(groups)),
@@ -480,13 +503,16 @@
                 pairs.append((m * groups + s, target * groups + m // ratio))
         arrived.append(lax.ppermute(sent, ("mp", "shot"), pairs))
     done = pl.pallas_call(
-        make_last_kernel(slabs, group, ratio),
+        make_last_kernel(slabs, group, groups),
         out_shape=jax.ShapeDtypeStruct((slab_rows * ratio, lines_z, width_y), jnp.float32),
         in_specs=[VMEM] * (slabs + 1),
         out_specs=VMEM,
+        scratch_shapes=[
+            pltpu.VMEM((slabs * group * lines_y, ratio * group * width_y), jnp.float32)
+        ],
         compiler_params=GRANT,
         name="smooth_y",
-    )(*arrived, last)
+    )(*arrived, table_y)
     return raw, jnp.swapaxes(done, 1, 2)
 
 
@@ -507,11 +533,11 @@
     first_row = lax.axis_index("mp") * slab_rows
     old_fwd, now_fwd = forward_old[0], forward_now[0]
     late_adj, now_adj = adjoint_late[0], adjoint_now[0]
-    tables = [jnp.asarray(table) for table in stencil_tables(shape[1], shape[2])]
+    tables = stencil_tables(shape[1], shape[2])
 
     signed = (2 * src_sign[0] - 1).astype(jnp.float32)
     halo_low, halo_high = exchange(*pack_edges(now_fwd, now_adj))
-    first_cell = (first_row * shape[1] * shape[2]).astype(jnp.int32).reshape(1)
+    first_cell = first_row * shape[1] * shape[2]
     source_0, source_1, data_0, data_1 = injections(
         (src_cell[0], signed * wavelet[0, 0], signed * wavelet[0, 1]),
         (rec_cell, rec_data[0, 0], rec_data[0, 1]),
@@ -531,7 +557,8 @@
         (courant, now_adj, accel, source_1, data_1), tables,
     )
     inner = sum_groups(term[REACH:-REACH])
-    outer = sum_groups(second_edges(halo_low, halo_high, courant, accel, mid_adj, term))
+    edges = second_edges(halo_low, halo_high, courant, accel, mid_adj, term)
+    outer = sum_groups(edges)
     return smooth(inner, outer, shape[0], shape[1], shape[2])
 
 

time: 162 us -> 160 us (0.988)
  the two profiles are of different devices: /device:TPU:10 before, /device:TPU:14 now
where the time goes in v1:
time: 160 us; the launch traced here: 159 us
  Pallas kernels  64.8 us (40%)
  waiting for transfers between devices  39.6 us (25%)
  starting transfers between devices  26.7 us (17%)
  local copies, waits for them, and re-layouts  22.9 us (14%)
  other arithmetic  4.44 us (3%)
    pallas_call x2, Pallas kernels, slab_step(): pl.pallas_call(kernel, grid=(blocks,), out_shape=(shape,) * outs, in_spec...  30.4 us
    pallas_call x1, Pallas kernels, injections(): pl.pallas_call(scatter_kernel, out_shape=(flat,) * 4, in_specs=[pl.BlockS...  18 us
    unnamed x38, local copies, waits for them, and re-layouts  17.8 us
    ppermute x4, waiting for transfers between devices, smooth(): arrived.append(lax.ppermute(sent, ('mp', 'shot'), pairs))  17.1 us
    ppermute x4, waiting for transfers between devices, sum_groups(): sent = lax.ppermute(other, 'shot', [(i, i ^ bit) for i in range(count)])  16.2 us
    ppermute x4, starting transfers between devices, smooth(): arrived.append(lax.ppermute(sent, ('mp', 'shot'), pairs))  7.35 us
    ppermute x2, starting transfers between devices, exchange(): from_low = lax.ppermute(high_edge, 'mp', upward)  6.87 us
    ppermute x2, starting transfers between devices, exchange(): from_high = lax.ppermute(low_edge, 'mp', downward)  5.84 us
  transfers between devices with their start and end apart: 15, of which 10 were waited for; matrix products, arithmetic and copies ran while one was open for 6% of the time, Pallas kernels for 32%

profile of v1, /device:TPU:14, one launch (start us, length us, event | category | flops | bytes accessed | tf_op | source)
XLA Modules:
  0.0 159.4 jit_solution(9605797123444608833)
XLA Ops:
  0.7 2.9 %pack_edges.1 = (f32[2,4,256,128]{3,2,1,0:T(8,128)}, f32[2,4,256,128]{3,2,1,0:T(8,128)}) custom-call(f32[24,256,128]{2,1,0:T(8,128)} %bitcast.63, f32[24,256,128]{2,1,0:T(8,128)} %bitcast.64, f32[24,256,128]{2,1,0:T(8,128)} %bitcast.66, f32[24,256,128]{2,1,0:T(8,128)} %bitcast.67), custom_call_target="tpu_custom_call" | custom-call | tf_op jit(solution)/shard_map/pack_edges/pallas_call | solution.py:311
  3.6 3.5 %collective-permute-start = (f32[2,4,256,128]{3,2,1,0:T(8,128)}, f32[2,4,256,128]{3,2,1,0:T(8,128)S(1)}, u32[]{:S(2)}, u32[]{:S(2)}) collective-permute-start(f32[2,4,256,128]{3,2,1,0:T(8,128)} %get-tuple-element.22), channel_id=1, source_target_pairs={{0,4},{4,8},{8,12},{1,5},{5,9},{9,13},{2,6},{6,10},{10,14},{3,7},{... | collective-permute-start | bytes 3145736 | tf_op jit(solution)/shard_map/ppermute | solution.py:326
  7.1 2.4 %collective-permute-start.1 = (f32[2,4,256,128]{3,2,1,0:T(8,128)}, f32[2,4,256,128]{3,2,1,0:T(8,128)S(1)}, u32[]{:S(2)}, u32[]{:S(2)}) collective-permute-start(f32[2,4,256,128]{3,2,1,0:T(8,128)} %get-tuple-element.23), channel_id=1, source_target_pairs={{4,0},{8,4},{12,8},{5,1},{9,5},{13,9},{6,2},{10,6},{14,10},{7,3},{... | collective-permute-start | bytes 3145736 | tf_op jit(solution)/shard_map/ppermute | solution.py:327
  12.5 18.0 %inject.1 = (f32[6144,128]{1,0:T(8,128)}, f32[6144,128]{1,0:T(8,128)}, f32[6144,128]{1,0:T(8,128)}, f32[6144,128]{1,0:T(8,128)}) custom-call(s32[2048]{0:T(1024)} %get-tuple-element.56.rec_row, s32[2048]{0:T(1024)} %get-tuple-element.55.rec_lane, f32[2048]{0:T(1024)} %get-tuple-element.54.rec_first, f32[2048]{0:T(1024)} %get-tuple-element.53.rec_second, ...), custom_call_target="tpu_custom_call" | custom-call | bytes 41943040 | tf_op jit(solution)/shard_map/inject/pallas_call | solution.py:100
  30.5 15.9 %shard_map.167 = (f32[24,256,128]{2,1,0:T(8,128)}, f32[24,256,128]{2,1,0:T(8,128)}, f32[24,256,128]{2,1,0:T(8,128)}) custom-call(f32[24,256,128]{2,1,0:T(8,128)} %bitcast.65, f32[24,256,128]{2,1,0:T(8,128)} %bitcast.68, f32[24,256,128]{2,1,0:T(8,128)} %courant.7, f32[24,256,128]{2,1,0:T(8,128)} %bitcast.75, f32[24,256,128]{2,1,0:T(8,128)} %bitcast.76, ...), custom_call_target="tpu_custom_call" | custom-call | flops 8589934592 | bytes 41943040 | tf_op jit(solution)/shard_map/pallas_call | solution.py:198
  48.3 1.9 %copy-done.4 = f32[24,256,128]{2,1,0:T(8,128)S(1)} copy-done((f32[24,256,128]{2,1,0:T(8,128)S(1)}, f32[24,256,128]{2,1,0:T(8,128)}, u32[]{:S(2)}) %copy-start.4) | copy-done | bytes 3145752
  50.2 1.9 %copy-done.7 = f32[24,256,128]{2,1,0:T(8,128)S(1)} copy-done((f32[24,256,128]{2,1,0:T(8,128)S(1)}, f32[24,256,128]{2,1,0:T(8,128)}, u32[]{:S(2)}) %copy-start.7) | copy-done | bytes 3145752
  52.1 3.3 %first_edges.1 = (f32[24,256,128]{2,1,0:T(8,128)S(1)}, f32[24,256,128]{2,1,0:T(8,128)S(1)}, f32[24,256,128]{2,1,0:T(8,128)S(1)}, f32[2,4,256,128]{3,2,1,0:T(8,128)}, f32[2,4,256,128]{3,2,1,0:T(8,128)}) custom-call(f32[2,4,256,128]{3,2,1,0:T(8,128)S(1)} %collective-permute-done.halo_low, ...), custom_call_target="tpu_custom_call", output_to_operand_aliasing={{0}: (3, {}), {1}: (4, {}), {2}: (5, {})} | custom-call | tf_op jit(solution)/shard_map/first_edges/pallas_call | solution.py:273
  60.5 3.4 %collective-permute-start.4 = (f32[2,4,256,128]{3,2,1,0:T(8,128)}, f32[2,4,256,128]{3,2,1,0:T(8,128)}, u32[]{:S(2)}, u32[]{:S(2)}) collective-permute-start(f32[2,4,256,128]{3,2,1,0:T(8,128)} %get-tuple-element.34), channel_id=1, source_target_pairs={{0,4},{4,8},{8,12},{1,5},{5,9},{9,13},{2,6},{6,10},{10,14},{3,7},{... | collective-permute-start | bytes 3145736 | tf_op jit(solution)/shard_map/ppermute | solution.py:326
  63.9 3.4 %collective-permute-start.5 = (f32[2,4,256,128]{3,2,1,0:T(8,128)}, f32[2,4,256,128]{3,2,1,0:T(8,128)}, u32[]{:S(2)}, u32[]{:S(2)}) collective-permute-start(f32[2,4,256,128]{3,2,1,0:T(8,128)} %get-tuple-element.35), channel_id=1, source_target_pairs={{4,0},{8,4},{12,8},{5,1},{9,5},{13,9},{6,2},{10,6},{14,10},{7,3},{... | collective-permute-start | bytes 3145736 | tf_op jit(solution)/shard_map/ppermute | solution.py:327
  67.3 14.5 %shard_map.168.term = f32[24,256,128]{2,1,0:T(8,128)} custom-call(f32[24,256,128]{2,1,0:T(8,128)} %copy-done.8, f32[24,256,128]{2,1,0:T(8,128)} %copy-done.5, f32[24,256,128]{2,1,0:T(8,128)} %courant.7, f32[24,256,128]{2,1,0:T(8,128)} %bitcast.69, f32[24,256,128]{2,1,0:T(8,128)} %copy-done.2, f32[24,256,128]{2,1,0:T(8,128)} %bitcast.77, ...), custom_call_target="tpu_custom_call" | custom-call | flops 8589934592 | bytes 41943040 | tf_op jit(solution)/shard_map/pallas_call | solution.py:198
  87.0 3.2 %collective-permute-done.5.halo_high = f32[2,4,256,128]{3,2,1,0:T(8,128)} collective-permute-done((f32[2,4,256,128]{3,2,1,0:T(8,128)}, f32[2,4,256,128]{3,2,1,0:T(8,128)}, u32[]{:S(2)}, u32[]{:S(2)}) %collective-permute-start.5) | collective-permute-done | bytes 1048608 | tf_op jit(solution)/shard_map/ppermute | solution.py:327
  90.2 1.9 %copy-done.3 = f32[24,256,128]{2,1,0:T(8,128)S(1)} copy-done((f32[24,256,128]{2,1,0:T(8,128)S(1)}, f32[24,256,128]{2,1,0:T(8,128)}, u32[]{:S(2)}) %copy-start.3) | copy-done | bytes 3145752
  93.9 2.3 %second_edges.1 = f32[8,256,128]{2,1,0:T(8,128)S(1)} custom-call(f32[2,4,256,128]{3,2,1,0:T(8,128)} %collective-permute-done.4.halo_low, f32[2,4,256,128]{3,2,1,0:T(8,128)} %collective-permute-done.5.halo_high, f32[24,256,128]{2,1,0:T(8,128)S(1)} %copy-done, f32[24,256,128]{2,1,0:T(8,128)S(1)} %copy-done.3, f32[24,256,128]{2,1,0:T(8,128)S(1)} %copy-done.6, ...), custom_call_target="tpu_custom_call" | custom-call | tf_op jit(solution)/shard_map/second_edges/pallas_call | solution.py:288
  102.5 12.1 %collective-permute-done.3 = f32[16,1,64,128]{3,2,0,1:T(8,128)S(1)} collective-permute-done((f32[16,1,64,128]{3,2,0,1:T(8,128)}, f32[16,1,64,128]{3,2,0,1:T(8,128)S(1)}, u32[]{:S(2)}, u32[]{:S(2)}) %collective-permute-start.3) | collective-permute-done | bytes 524320 | tf_op jit(solution)/shard_map/ppermute | solution.py:342
  114.7 4.1 %collective-permute-done.7 = f32[8,1,64,128]{3,2,0,1:T(8,128)S(1)} collective-permute-done((f32[8,1,64,128]{3,2,0,1:T(8,128)S(1)}, f32[8,1,64,128]{3,2,0,1:T(8,128)S(1)}, u32[]{:S(2)}, u32[]{:S(2)}) %collective-permute-start.7) | collective-permute-done | bytes 262176 | tf_op jit(solution)/shard_map/ppermute | solution.py:342
  122.5 2.4 %collective-permute-start.9 = (f32[1,64,128]{2,1,0:T(8,128)S(1)}, f32[1,64,128]{2,1,0:T(8,128)S(1)}, u32[]{:S(2)}, u32[]{:S(2)}) collective-permute-start(f32[1,64,128]{2,1,0:T(8,128)S(1)} %get-tuple-element.49), channel_id=1, source_target_pairs={{0,8},{4,12},{8,0},{12,4},{1,9},{5,13},{9,1},{13,5},{2,10},{6,14},... | collective-permute-start | bytes 98312 | tf_op jit(solution)/shard_map/ppermute | solution.py:486
  128.5 4.0 %smooth_xz.1 = (f32[12,32,128]{2,1,0:T(8,128)S(1)}, f32[12,32,128]{2,1,0:T(8,128)S(1)}, f32[12,32,128]{2,1,0:T(8,128)S(1)}, f32[12,32,128]{2,1,0:T(8,128)S(1)}) custom-call(f32[24,64,128]{2,1,0:T(8,128)S(1)} %copy-done.9, f32[1,64,128]{2,1,0:T(8,128)S(1)} %collective-permute-done.8.refs_0_, f32[1,64,128]{2,1,0:T(8,128)S(1)} %collective-permute-done.9.refs_1_, ...), custom_call_target="tpu_custom_call" | custom-call | tf_op jit(solution)/shard_map/smooth_xz/pallas_call | solution.py:488
  132.5 1.9 %collective-permute-start.11 = (f32[12,32,128]{2,1,0:T(8,128)S(1)}, f32[12,32,128]{2,1,0:T(8,128)S(1)}, u32[]{:S(2)}, u32[]{:S(2)}) collective-permute-start(f32[12,32,128]{2,1,0:T(8,128)S(1)} %get-tuple-element.38), channel_id=1, source_target_pairs={{0,0},{1,4},{2,8},{3,12},{4,1},{5,5},{6,9},{7,13},{8,2},{9,6},{10,... | collective-permute-start | bytes 589832 | tf_op jit(solution)/shard_map/ppermute | solution.py:504
  134.7 5.1 %collective-permute-start.13 = (f32[12,32,128]{2,1,0:T(8,128)S(1)}, f32[12,32,128]{2,1,0:T(8,128)S(1)}, u32[]{:S(2)}, u32[]{:S(2)}) collective-permute-start(f32[12,32,128]{2,1,0:T(8,128)S(1)} %get-tuple-element.40), channel_id=1, source_target_pairs={{0,8},{1,12},{2,0},{3,4},{4,9},{5,13},{6,1},{7,5},{8,10},{9,14},{1... | collective-permute-start | bytes 589832 | tf_op jit(solution)/shard_map/ppermute | solution.py:504
  139.9 7.6 %collective-permute-done.11.refs_0_ = f32[12,32,128]{2,1,0:T(8,128)S(1)} collective-permute-done((f32[12,32,128]{2,1,0:T(8,128)S(1)}, f32[12,32,128]{2,1,0:T(8,128)S(1)}, u32[]{:S(2)}, u32[]{:S(2)}) %collective-permute-start.11) | collective-permute-done | bytes 196640 | tf_op jit(solution)/shard_map/ppermute | solution.py:504
  147.5 5.6 %collective-permute-done.12.refs_1_ = f32[12,32,128]{2,1,0:T(8,128)S(1)} collective-permute-done((f32[12,32,128]{2,1,0:T(8,128)S(1)}, f32[12,32,128]{2,1,0:T(8,128)S(1)}, u32[]{:S(2)}, u32[]{:S(2)}) %collective-permute-start.12) | collective-permute-done | bytes 196640 | tf_op jit(solution)/shard_map/ppermute | solution.py:504
  153.0 2.3 %collective-permute-done.13.refs_2_ = f32[12,32,128]{2,1,0:T(8,128)S(1)} collective-permute-done((f32[12,32,128]{2,1,0:T(8,128)S(1)}, f32[12,32,128]{2,1,0:T(8,128)S(1)}, u32[]{:S(2)}, u32[]{:S(2)}) %collective-permute-start.13) | collective-permute-done | bytes 196640 | tf_op jit(solution)/shard_map/ppermute | solution.py:504
  157.0 2.4 %smooth_y.1 = f32[24,32,256]{2,1,0:T(8,128)} custom-call(f32[12,32,128]{2,1,0:T(8,128)S(1)} %collective-permute-done.11.refs_0_, f32[12,32,128]{2,1,0:T(8,128)S(1)} %collective-permute-done.12.refs_1_, f32[12,32,128]{2,1,0:T(8,128)S(1)} %collective-permute-done.13.refs_2_, f32[12,32,128]{2,1,0:T(8,128)S(1)} %collective-permute-done.14.refs_3_, ...), custom_call_target="tpu_custom_call" | custom-call | tf_op jit(solution)/shard_map/smooth_y/pallas_call | solution.py:505
  (73 shorter events, 32.6 us)
Async XLA Ops:
  0.6 8.9 %copy-start.14 = (f32[1,2,2048]{2,1,0:T(2,128)S(1)}, f32[1,2,2048]{2,1,0:T(2,128)}, u32[]{:S(2)}) copy-start(f32[1,2,2048]{2,1,0:T(2,128)} %param.25) | copy-start | bytes 49156
  0.6 8.9 %copy-start.15 = (s32[1,64]{1,0:T(1,128)S(1)}, s32[1,64]{1,0:T(1,128)}, u32[]{:S(2)}) copy-start(s32[1,64]{1,0:T(1,128)} %param.21) | copy-start | bytes 772
  0.7 9.5 %copy-start.13 = (s32[2048]{0:T(1024)S(1)}, s32[2048]{0:T(1024)}, u32[]{:S(2)}) copy-start(s32[2048]{0:T(1024)} %param.24) | copy-start | bytes 24580
  0.7 10.1 %copy-start.16 = (f32[1,2,64]{2,1,0:T(2,128)S(1)}, f32[1,2,64]{2,1,0:T(2,128)}, u32[]{:S(2)}) copy-start(f32[1,2,64]{2,1,0:T(2,128)} %param.23) | copy-start | bytes 1540
  0.7 10.1 %copy-start.17 = (s32[1,64]{1,0:T(1,128)S(1)}, s32[1,64]{1,0:T(1,128)}, u32[]{:S(2)}) copy-start(s32[1,64]{1,0:T(1,128)} %param.22) | copy-start | bytes 772
  3.6 42.8 %collective-permute-start = (f32[2,4,256,128]{3,2,1,0:T(8,128)}, f32[2,4,256,128]{3,2,1,0:T(8,128)S(1)}, u32[]{:S(2)}, u32[]{:S(2)}) collective-permute-start(f32[2,4,256,128]{3,2,1,0:T(8,128)} %get-tuple-element.22), channel_id=1, source_target_pairs={{0,4},{4,8},{8,12},{1,5},{5,9},{9,13},{2,6},{6,10},{10,14},{3,7},{... | collective-permute-start | bytes 3145736 | tf_op jit(solution)/shard_map/ppermute | solution.py:326
  7.1 39.3 %collective-permute-start.1 = (f32[2,4,256,128]{3,2,1,0:T(8,128)}, f32[2,4,256,128]{3,2,1,0:T(8,128)S(1)}, u32[]{:S(2)}, u32[]{:S(2)}) collective-permute-start(f32[2,4,256,128]{3,2,1,0:T(8,128)} %get-tuple-element.23), channel_id=1, source_target_pairs={{4,0},{8,4},{12,8},{5,1},{9,5},{13,9},{6,2},{10,6},{14,10},{7,3},{... | collective-permute-start | bytes 3145736 | tf_op jit(solution)/shard_map/ppermute | solution.py:327
  46.4 1.9 %copy-start.1 = (f32[24,256,128]{2,1,0:T(8,128)S(1)}, f32[24,256,128]{2,1,0:T(8,128)}, u32[]{:S(2)}) copy-start(f32[24,256,128]{2,1,0:T(8,128)} %get-tuple-element.26.accel_in) | copy-start | bytes 9437188
  60.5 26.5 %collective-permute-start.4 = (f32[2,4,256,128]{3,2,1,0:T(8,128)}, f32[2,4,256,128]{3,2,1,0:T(8,128)}, u32[]{:S(2)}, u32[]{:S(2)}) collective-permute-start(f32[2,4,256,128]{3,2,1,0:T(8,128)} %get-tuple-element.34), channel_id=1, source_target_pairs={{0,4},{4,8},{8,12},{1,5},{5,9},{9,13},{2,6},{6,10},{10,14},{3,7},{... | collective-permute-start | bytes 3145736 | tf_op jit(solution)/shard_map/ppermute | solution.py:326
  63.9 26.3 %collective-permute-start.5 = (f32[2,4,256,128]{3,2,1,0:T(8,128)}, f32[2,4,256,128]{3,2,1,0:T(8,128)}, u32[]{:S(2)}, u32[]{:S(2)}) collective-permute-start(f32[2,4,256,128]{3,2,1,0:T(8,128)} %get-tuple-element.35), channel_id=1, source_target_pairs={{4,0},{8,4},{12,8},{5,1},{9,5},{13,9},{6,2},{10,6},{14,10},{7,3},{... | collective-permute-start | bytes 3145736 | tf_op jit(solution)/shard_map/ppermute | solution.py:327
  83.4 6.8 %copy-start = (f32[24,256,128]{2,1,0:T(8,128)S(1)}, f32[24,256,128]{2,1,0:T(8,128)}, u32[]{:S(2)}) copy-start(f32[24,256,128]{2,1,0:T(8,128)} %courant.7) | copy-start | bytes 9437188
  85.6 10.9 %collective-permute-start.2 = (f32[16,2,64,128]{3,2,0,1:T(8,128)}, f32[16,2,64,128]{3,2,0,1:T(8,128)}, u32[]{:S(2)}, u32[]{:S(2)}) collective-permute-start(f32[16,2,64,128]{3,2,0,1:T(8,128)} %bitcast.60), channel_id=1, source_target_pairs={{0,1},{1,0},{2,3},{3,2},{4,5},{5,4},{6,7},{7,6},{8,9},{9,8},{10,11... | collective-permute-start | bytes 3145736 | tf_op jit(solution)/shard_map/ppermute | solution.py:342
  96.3 3.9 %copy-start.12 = (f32[256,128]{1,0:T(8,128)S(1)}, f32[256,128]{1,0:T(8,128)}, u32[]{:S(2)}) copy-start(f32[256,128]{1,0:T(8,128)} %constant.174.clone) | copy-start | bytes 393220
  96.4 3.8 %collective-permute-start.6 = (f32[8,2,64,128]{3,2,0,1:T(8,128)S(1)}, f32[8,2,64,128]{3,2,0,1:T(8,128)S(1)}, u32[]{:S(2)}, u32[]{:S(2)}) collective-permute-start(f32[8,2,64,128]{3,2,0,1:T(8,128)S(1)} %bitcast.72), channel_id=1, source_target_pairs={{0,1},{1,0},{2,3},{3,2},{4,5},{5,4},{6,7},{7,6},{8,9},{9,8},{10,11... | collective-permute-start | bytes 1572872 | tf_op jit(solution)/shard_map/ppermute | solution.py:342
  99.6 15.0 %collective-permute-start.3 = (f32[16,1,64,128]{3,2,0,1:T(8,128)}, f32[16,1,64,128]{3,2,0,1:T(8,128)S(1)}, u32[]{:S(2)}, u32[]{:S(2)}) collective-permute-start(f32[16,1,64,128]{3,2,0,1:T(8,128)} %constant_dynamic-slice_fusion.8), channel_id=1, source_target_pairs={{0,2},{1,3},{2,0},{3,1},{4,6},{5,7},{6,4},{7,5},{8,10},{9,11},{10,... | collective-permute-start | bytes 1572872 | tf_op jit(solution)/shard_map/ppermute | solution.py:342
  100.2 56.8 %copy-start.10 = (f32[256,256]{1,0:T(8,128)S(1)}, f32[256,256]{1,0:T(8,128)}, u32[]{:S(2)}) copy-start(f32[256,256]{1,0:T(8,128)} %constant.175.clone.refs_4_) | copy-start | bytes 786436
  100.3 18.5 %collective-permute-start.7 = (f32[8,1,64,128]{3,2,0,1:T(8,128)S(1)}, f32[8,1,64,128]{3,2,0,1:T(8,128)S(1)}, u32[]{:S(2)}, u32[]{:S(2)}) collective-permute-start(f32[8,1,64,128]{3,2,0,1:T(8,128)S(1)} %constant_dynamic-slice_fusion.5), channel_id=1, source_target_pairs={{0,2},{1,3},{2,0},{3,1},{4,6},{5,7},{6,4},{7,5},{8,10},{9,11},{10,... | collective-permute-start | bytes 786440 | tf_op jit(solution)/shard_map/ppermute | solution.py:342
  120.4 5.2 %collective-permute-start.10 = (f32[1,64,128]{2,1,0:T(8,128)S(1)}, f32[1,64,128]{2,1,0:T(8,128)S(1)}, u32[]{:S(2)}, u32[]{:S(2)}) collective-permute-start(f32[1,64,128]{2,1,0:T(8,128)S(1)} %get-tuple-element.48), channel_id=1, source_target_pairs={{0,12},{4,0},{8,4},{12,8},{1,13},{5,1},{9,5},{13,9},{2,14},{6,2},{... | collective-permute-start | bytes 98312 | tf_op jit(solution)/shard_map/ppermute | solution.py:486
  122.0 3.9 %collective-permute-start.8 = (f32[1,64,128]{2,1,0:T(8,128)S(1)}, f32[1,64,128]{2,1,0:T(8,128)S(1)}, u32[]{:S(2)}, u32[]{:S(2)}) collective-permute-start(f32[1,64,128]{2,1,0:T(8,128)S(1)} %get-tuple-element.50), channel_id=1, source_target_pairs={{0,4},{4,8},{8,12},{12,0},{1,5},{5,9},{9,13},{13,1},{2,6},{6,10},{... | collective-permute-start | bytes 98312 | tf_op jit(solution)/shard_map/ppermute | solution.py:486
  122.5 4.8 %collective-permute-start.9 = (f32[1,64,128]{2,1,0:T(8,128)S(1)}, f32[1,64,128]{2,1,0:T(8,128)S(1)}, u32[]{:S(2)}, u32[]{:S(2)}) collective-permute-start(f32[1,64,128]{2,1,0:T(8,128)S(1)} %get-tuple-element.49), channel_id=1, source_target_pairs={{0,8},{4,12},{8,0},{12,4},{1,9},{5,13},{9,1},{13,5},{2,10},{6,14},... | collective-permute-start | bytes 98312 | tf_op jit(solution)/shard_map/ppermute | solution.py:486
  132.5 14.9 %collective-permute-start.11 = (f32[12,32,128]{2,1,0:T(8,128)S(1)}, f32[12,32,128]{2,1,0:T(8,128)S(1)}, u32[]{:S(2)}, u32[]{:S(2)}) collective-permute-start(f32[12,32,128]{2,1,0:T(8,128)S(1)} %get-tuple-element.38), channel_id=1, source_target_pairs={{0,0},{1,4},{2,8},{3,12},{4,1},{5,5},{6,9},{7,13},{8,2},{9,6},{10,... | collective-permute-start | bytes 589832 | tf_op jit(solution)/shard_map/ppermute | solution.py:504
  134.4 18.6 %collective-permute-start.12 = (f32[12,32,128]{2,1,0:T(8,128)S(1)}, f32[12,32,128]{2,1,0:T(8,128)S(1)}, u32[]{:S(2)}, u32[]{:S(2)}) collective-permute-start(f32[12,32,128]{2,1,0:T(8,128)S(1)} %get-tuple-element.39), channel_id=1, source_target_pairs={{0,4},{1,8},{2,12},{3,0},{4,5},{5,9},{6,13},{7,1},{8,6},{9,10},{10... | collective-permute-start | bytes 589832 | tf_op jit(solution)/shard_map/ppermute | solution.py:504
  134.7 20.6 %collective-permute-start.13 = (f32[12,32,128]{2,1,0:T(8,128)S(1)}, f32[12,32,128]{2,1,0:T(8,128)S(1)}, u32[]{:S(2)}, u32[]{:S(2)}) collective-permute-start(f32[12,32,128]{2,1,0:T(8,128)S(1)} %get-tuple-element.40), channel_id=1, source_target_pairs={{0,8},{1,12},{2,0},{3,4},{4,9},{5,13},{6,1},{7,5},{8,10},{9,14},{1... | collective-permute-start | bytes 589832 | tf_op jit(solution)/shard_map/ppermute | solution.py:504
  139.8 17.1 %collective-permute-start.14 = (f32[12,32,128]{2,1,0:T(8,128)S(1)}, f32[12,32,128]{2,1,0:T(8,128)S(1)}, u32[]{:S(2)}, u32[]{:S(2)}) collective-permute-start(f32[12,32,128]{2,1,0:T(8,128)S(1)} %get-tuple-element.41), channel_id=1, source_target_pairs={{0,12},{1,0},{2,4},{3,8},{4,13},{5,1},{6,5},{7,9},{8,14},{9,2},{10... | collective-permute-start | bytes 589832 | tf_op jit(solution)/shard_map/ppermute | solution.py:504
  (10 other events, 16.6 us)
